TPU v7x, 256 devices: a whole 4x4x8 slice. The times are simulated.
256 devices in a mesh: bead: 32 (over y, z), space: 8 (over x, core).
Axes of the slice: x: 4, y: 4, z: 8, core: 2. Of those that a mesh axis runs over, the one named last changes fastest.
Arguments:
- positions: float32 [32, 3, 131072], P('bead', None, 'space'), may hold values from -5.5 to 5.5
- charges: float32 [131072], P('space'), may hold values from -1 to 1
- polarizability: float32 [131072], P('space'), may hold values from 0.03 to 0.12
- masses: float32 [131072], P('space'), may hold values from 1 to 16
- neighbors: int32 [1024, 8], P('space'), may hold values from 0 to 135, as said below
Outputs:
- forces: float32 [32, 3, 131072], P('bead', None, 'space')
- dipoles: float32 [3, 131072], P(None, ('space', 'bead'))
Inputs may be any that keep to these rules, and one draw needn't show every extreme that they name: `neighbors`: row t lists 8 different tiles by their index in its domain's extended numbering: the last 4 tiles of the previous domain, the domain's own 128 tiles, the first 4 tiles of the next domain (domains form a cycle). Every listed tile lies within 4 tiles of tile t, and the two tiles at distance exactly 4 on either side are always listed.
All inputs are finite; a program needn't handle non-finite values.
Results may differ from a plain program's by a relative error of at most 0.0001.
Values sent between devices are 32-bit elements; how exact they have to be, the bound alone decides.
No kernel may reach another device: no remote copies, remote signals or barrier semaphores. Data moves between devices by JAX's collectives and lax.ppermute only.
A program may use at most 64 MiB of HBM per device.

v0:
```python
import math
import jax
import jax.numpy as jnp
from jax import lax
from jax.sharding import PartitionSpec as P

TILE = 128
HALO_T = 4
ITERS = 3
REPULSION = 0.2
SPRING = 0.1


def extended_2(value, sides, width):
    for axis, dim in sides:
        size, length = (lax.axis_size(axis), value.shape[dim])
        up = [(i, (i + 1) % size) for i in range(size)]
        down = [(j, i) for i, j in up]
        last = lax.slice_in_dim(value, length - width, length, axis=dim)
        first = lax.slice_in_dim(value, 0, width, axis=dim)
        before = lax.ppermute(last, axis, up)
        after = lax.ppermute(first, axis, down)
        value = jnp.concatenate([before, value, after], axis=dim)
    return value


def repulsion_kernel(targets, sources):
    displace = targets[:, :, :, None] - sources[:, :, None, :]
    weight = jnp.exp(-0.5 * jnp.sum(displace * displace, axis=0))
    return REPULSION * jnp.sum(weight[None] * displace, axis=3)


def charge_kernel(targets, sources, charge):
    displace = targets[:, :, :, None] - sources[:, :, None, :]
    weight = jnp.exp(-0.25 * jnp.sum(displace * displace, axis=0)) * charge[0][:, None, :]
    return jnp.sum(weight[None] * displace, axis=3)


def dipole_kernel(targets, sources, dipole):
    displace = targets[:, :, :, None] - sources[:, :, None, :]
    weight = jnp.exp(-0.25 * jnp.sum(displace * displace, axis=0))
    spread_dip = dipole[:, :, None, :]
    projected = jnp.sum(displace * spread_dip, axis=0)
    return jnp.sum(weight[None] * (0.25 * displace * projected[None] - 0.5 * spread_dip), axis=3)


def grouped(kernel, targets, sources):
    tile_count = targets.shape[1]
    group_size = math.gcd(tile_count, 4)

    def split_tiles(tensor):
        return jnp.moveaxis(
            tensor.reshape(tensor.shape[0], tile_count // group_size, group_size, tensor.shape[2]),
            1,
            0,
        )

    pieces = tuple((split_tiles(tensor) for tensor in (targets,) + tuple(sources)))
    result = lax.map(lambda member: kernel(*member), pieces)
    return jnp.moveaxis(result, 0, 1).reshape(3, tile_count, targets.shape[2])


def gather_local(extended, tile_rows):
    channels = extended.shape[0]
    tiles = extended.reshape(channels, extended.shape[1] // TILE, TILE)
    picked = jnp.take(tiles, tile_rows, axis=1)
    return picked.reshape(channels, tile_rows.shape[0], tile_rows.shape[1] * TILE)


def per_device(positions, charges, polarizability, masses, neighbors):
    coords = positions[0]
    atom_dev = coords.shape[1]
    rim_width = HALO_T * TILE
    tiles_domain = atom_dev // TILE
    beads = lax.axis_size("bead")
    bead_index = lax.axis_index("bead")
    own_tiles = tiles_domain // beads
    own_start = bead_index * own_tiles
    cycle_rows = extended_2(positions, (("bead", 0),), 1)
    spring = SPRING * masses[None, :] * (cycle_rows[0] + cycle_rows[2] - 2.0 * coords)
    extended = extended_2(coords, (("space", 1),), rim_width)
    targets = coords.reshape(3, tiles_domain, TILE)
    short_range = grouped(repulsion_kernel, targets, (gather_local(extended, neighbors),)).reshape(
        3, atom_dev
    )
    centroid = lax.psum(coords, "bead") / beads
    with_charge = jnp.concatenate([centroid, charges[None]], axis=0)
    cent_ext = extended_2(with_charge, (("space", 1),), rim_width)
    cent_tiles = centroid.reshape(3, tiles_domain, TILE)
    cent_sources = gather_local(cent_ext[:3], neighbors)
    charge_sources = gather_local(cent_ext[3:], neighbors)
    permanent = grouped(charge_kernel, cent_tiles, (cent_sources, charge_sources)).reshape(
        3, atom_dev
    )

    def induced(dipole_all):
        wide_dip = extended_2(dipole_all, (("space", 1),), rim_width)
        field = grouped(
            dipole_kernel, cent_tiles, (cent_sources, gather_local(wide_dip, neighbors))
        )
        return field.reshape(3, atom_dev)

    domain_dip = polarizability[None] * permanent
    for sweep_index in range(ITERS):
        domain_dip = polarizability[None] * (permanent + induced(domain_dip))
    pulled = charges[None] * induced(domain_dip)
    dipoles = lax.dynamic_slice_in_dim(domain_dip, own_start * TILE, own_tiles * TILE, 1)
    forces = (short_range + spring + pulled)[None]
    return (forces, dipoles)


def solution(mesh):
    in_specs = (P("bead", None, "space"), P("space"), P("space"), P("space"), P("space", None))
    out_specs = (P("bead", None, "space"), P(None, ("space", "bead")))
    return jax.shard_map(
        per_device, mesh=mesh, in_specs=in_specs, out_specs=out_specs, check_vma=False
    )
```

profile of v0, /device:TPU:7, one launch (start us, length us, event | category | flops | bytes accessed | tf_op | source)
XLA Modules:
  0.0 1015.9 jit_solution(263732601985356042)
XLA Ops:
  8.3 2.5 collective-permute-start
  11.6 3.4 collective-permute-done.1
  15.9 145.2 %all-reduce.2.cloned.1.call-done = f32[3,16384]{1,0:T(4,128)} async-done(((f32[3,16384]{1,0:T(4,128)}), f32[3,16384]{1,0:T(4,128)}) %all-reduce.2.cloned.1.call-update) | async-done | bytes 196624 | tf_op jit(solution)/shard_map/psum | solution.py:86
  162.8 5.3 collective-permute-start.4
  169.2 3.6 gather_fusion.1
  173.3 2.8 gather_fusion
  177.1 8.0 gather_fusion.2
  185.1 3.6 fusion.29
  192.1 87.0 %while.61 = (s32[]{:T(128)}, f32[32,3,4,128]{3,2,1,0:T(4,128)S(1)}, f32[32,3,4,128]{3,2,1,0:T(4,128)S(1)}, f32[32,3,4,1024]{3,2,1,0:T(4,128)}, f32[32,1,4,1024]{3,2,1,0:T(4,128)S(1)}, /*index=5*/s32[]{:T(128)}) while((s32[]{:T(128)}, f32[32,3,4,128]{3,2,1,0:T(4,128)S(1)}, f32[32,3,4,128]{3,2,1,0:T(4,128)S(1)}, f32[32,3,4,1024]{3,2,1,0:T(4,128)}, ...), condition=%wide.region_8.10_spmd, body=%wide.region_5.9_spmd.sunk | while | flops 9959938 | bytes 8677469 | solution.py:59
  279.3 3.0 collective-permute-start.6
  283.1 3.5 collective-permute-done.7
  286.7 3.6 gather_fusion.3
  293.5 141.8 %while.62 = (s32[]{:T(128)}, f32[32,3,4,128]{3,2,1,0:T(4,128)S(1)}, f32[32,3,4,128]{3,2,1,0:T(4,128)S(1)}, f32[32,3,4,1024]{3,2,1,0:T(4,128)}, f32[32,3,4,1024]{3,2,0,1:T(4,128)S(1)}, /*index=5*/s32[]{:T(128)}) while((s32[]{:T(128)}, f32[32,3,4,128]{3,2,1,0:T(4,128)S(1)}, f32[32,3,4,128]{3,2,1,0:T(4,128)S(1)}, ...), condition=%wide.region_13.15_spmd, body=%wide.region_9.14_spmd.sunk | while | flops 15739394 | bytes 17262684 | solution.py:59
  436.5 4.4 collective-permute-start.3
  441.0 3.6 gather_fusion.4
  447.8 141.8 %while.63 = (s32[]{:T(128)}, f32[32,3,4,128]{3,2,1,0:T(4,128)S(1)}, f32[32,3,4,128]{3,2,1,0:T(4,128)S(1)}, f32[32,3,4,1024]{3,2,1,0:T(4,128)}, f32[32,3,4,1024]{3,2,0,1:T(4,128)S(1)}, /*index=5*/s32[]{:T(128)}) while((s32[]{:T(128)}, f32[32,3,4,128]{3,2,1,0:T(4,128)S(1)}, f32[32,3,4,128]{3,2,1,0:T(4,128)S(1)}, ...), condition=%wide.region_18.20_spmd, body=%wide.region_14.19_spmd.sunk | while | flops 15739394 | bytes 17262684 | solution.py:59
  590.0 3.1 collective-permute-start.10
  594.7 2.6 collective-permute-done.11
  597.4 3.6 gather_fusion.5
  604.1 141.8 %while.64 = (s32[]{:T(128)}, f32[32,3,4,128]{3,2,1,0:T(4,128)S(1)}, f32[32,3,4,128]{3,2,1,0:T(4,128)S(1)}, f32[32,3,4,1024]{3,2,1,0:T(4,128)}, f32[32,3,4,1024]{3,2,0,1:T(4,128)S(1)}, /*index=5*/s32[]{:T(128)}) while((s32[]{:T(128)}, f32[32,3,4,128]{3,2,1,0:T(4,128)S(1)}, f32[32,3,4,128]{3,2,1,0:T(4,128)S(1)}, ...), condition=%wide.region_23.25_spmd, body=%wide.region_19.24_spmd.sunk | while | flops 15739394 | bytes 17262684 | solution.py:59
  746.9 3.0 collective-permute-start.12
  749.9 107.9 %while.60 = (s32[]{:T(128)}, f32[32,3,4,128]{3,2,1,0:T(4,128)S(1)}, f32[32,3,4,128]{3,2,0,1:T(4,128)}, f32[32,3,4,1024]{3,2,0,1:T(4,128)}, s32[]{:T(128)}) while((s32[]{:T(128)}, f32[32,3,4,128]{3,2,1,0:T(4,128)S(1)}, f32[32,3,4,128]{3,2,0,1:T(4,128)}, f32[32,3,4,1024]{3,2,0,1:T(4,128)}, s32[]{:T(128)}) %tuple.164), condition=%wide.region_3.5_spmd, body=%wide.region_0.4_spmd.sunk | while | flops 9437186 | bytes 8628305 | solution.py:59
  857.9 3.6 gather_fusion.6
  864.7 142.0 %while.65 = (s32[]{:T(128)}, f32[32,3,4,128]{3,2,1,0:T(4,128)S(1)}, f32[32,3,4,128]{3,2,1,0:T(4,128)S(1)}, f32[32,3,4,1024]{3,2,1,0:T(4,128)}, f32[32,3,4,1024]{3,2,0,1:T(4,128)S(1)}, /*index=5*/s32[]{:T(128)}) while((s32[]{:T(128)}, f32[32,3,4,128]{3,2,1,0:T(4,128)S(1)}, f32[32,3,4,128]{3,2,1,0:T(4,128)S(1)}, ...), condition=%wide.region_28.30_spmd, body=%wide.region_24.29_spmd.sunk | while | flops 15739394 | bytes 17262684 | solution.py:59
  (1410 shorter events, 783.9 us)
Async XLA Ops:
  7.2 160.9 %copy-start.7 = (s32[128,8]{0,1:T(8,128)S(1)}, s32[128,8]{0,1:T(8,128)}, u32[]{:S(2)}) copy-start(s32[128,8]{0,1:T(8,128)} %param.23) | copy-start | bytes 12292
  8.2 6.9 copy-start.1
  8.3 3.4 collective-permute-start
  10.7 4.3 collective-permute-start.1
  15.1 146.0 %all-reduce.2.cloned.1.call-start = ((), (), s32[]{:S(2)}) async-start(), calls=%async_computation | async-start | bytes 524288 | tf_op jit(solution)/shard_map/psum | solution.py:86
  162.8 10.2 collective-permute-start.4
  168.1 4.9 collective-permute-start.5
  169.2 3.8 copy-start.3
  190.5 1.3 copy-start.2
  190.5 1.3 copy-start.5
  192.1 87.2 %copy-start.4 = (f32[16384]{0:T(1024)S(1)}, f32[16384]{0:T(1024)}, u32[]{:S(2)}) copy-start(f32[16384]{0:T(1024)} %param.21) | copy-start | bytes 196612
  279.3 3.8 collective-permute-start.6
  282.3 4.3 collective-permute-start.7
  435.6 5.3 collective-permute-start.8
  435.7 5.3 collective-permute-start.9
  436.1 570.7 %collective-permute-start.2 = (f32[1,3,16384]{2,0,1:T(1,128)}, f32[1,3,16384]{2,0,1:T(1,128)S(1)}, u32[]{:S(2)}, u32[]{:S(2)}) collective-permute-start(f32[1,3,16384]{2,0,1:T(1,128)} %param.19), channel_id=1, source_target_pairs={{0,8},{8,16},{16,24},{24,32},{32,40},{40,48},{48,56},{56,64},{64,7... | collective-permute-start | bytes 589832 | tf_op jit(solution)/shard_map/ppermute | solution.py:21
  436.5 570.3 %collective-permute-start.3 = (f32[1,3,16384]{2,0,1:T(1,128)}, f32[1,3,16384]{2,0,1:T(1,128)}, u32[]{:S(2)}, u32[]{:S(2)}) collective-permute-start(f32[1,3,16384]{2,0,1:T(1,128)} %param.19), channel_id=1, source_target_pairs={{8,0},{16,8},{24,16},{32,24},{40,32},{48,40},{56,48},{64,56},{72,6... | collective-permute-start | bytes 589832 | tf_op jit(solution)/shard_map/ppermute | solution.py:22
  447.8 145.2 %copy-start.6 = (f32[16384]{0:T(1024)S(1)}, f32[16384]{0:T(1024)}, u32[]{:S(2)}) copy-start(f32[16384]{0:T(1024)} %param.22) | copy-start | bytes 196612
  589.6 3.4 copy-start
  590.0 4.7 collective-permute-start.10
  593.0 4.3 collective-permute-start.11
  746.9 111.0 %collective-permute-start.13 = (f32[3,512]{1,0:T(4,128)S(1)}, f32[3,512]{1,0:T(4,128)S(1)}, u32[]{:S(2)}, u32[]{:S(2)}) collective-permute-start(f32[3,512]{1,0:T(4,128)S(1)} %get-tuple-element.309), channel_id=1, source_target_pairs={{1,0},{2,1},{3,2},{4,3},{5,4},{6,5},{7,6},{0,7},{9,8},{10,9},{11,1... | collective-permute-start | bytes 18440 | tf_op jit(solution)/shard_map/ppermute | solution.py:22
  746.9 111.0 %collective-permute-start.12 = (f32[3,512]{1,0:T(4,128)S(1)}, f32[3,512]{1,0:T(4,128)S(1)}, u32[]{:S(2)}, u32[]{:S(2)}) collective-permute-start(f32[3,512]{1,0:T(4,128)S(1)} %get-tuple-element.310), channel_id=1, source_target_pairs={{0,1},{1,2},{2,3},{3,4},{4,5},{5,6},{6,7},{7,0},{8,9},{9,10},{10,1... | collective-permute-start | bytes 18440 | tf_op jit(solution)/shard_map/ppermute | solution.py:21
Sparse Core Ops, SparseCore 0:
  19.4 141.6 all-reduce.1
where the time goes:
time: 1030 us; the launch traced here: 1020 us
  other arithmetic  587 us (57%)
  local copies, waits for them, and re-layouts  227 us (22%)
  waiting for transfers between devices  156 us (15%)
  starting transfers between devices  22.1 us (2%)
  between operations  14.6 us (1%)
    reduce_sum x128, other arithmetic, dipole_kernel(): jnp.sum(weight[None] * (0.25 * displace * projected[None] - 0.5 * spread_...  199 us
    psum x1, waiting for transfers between devices, per_device(): centroid = lax.psum(coords, 'bead') / beads  145 us
    reduce_sum x128, other arithmetic, dipole_kernel(): weight = jnp.exp(-0.25 * jnp.sum(displace * displace, axis=0))  135 us
    exp x128, other arithmetic, dipole_kernel(): weight = jnp.exp(-0.25 * jnp.sum(displace * displace, axis=0))  119 us
    sub x256, local copies, waits for them, and re-layouts, dipole_kernel(): displace = targets[:, :, :, None] - sources[:, :, None, :]  105 us
    sub x64, local copies, waits for them, and re-layouts, repulsion_kernel(): displace = targets[:, :, :, None] - sources[:, :, None, :]  48 us
    gather x8, local copies, waits for them, and re-layouts, gather_local(): picked = jnp.take(tiles, tile_rows, axis=1)  29.6 us
    reduce_sum x32, other arithmetic, repulsion_kernel(): return REPULSION * jnp.sum(weight[None] * displace, axis=3)  27.5 us
  transfers between devices with their start and end apart: 15, of which 5 were waited for; matrix products, arithmetic and copies ran while one was open for 55% of the time, Pallas kernels for 0%

commit v1 on v0

--- a/solution.py
+++ b/solution.py
@@ -9,6 +9,12 @@
 ITERS = 3
 REPULSION = 0.2
 SPRING = 0.1
+
+
+def gather_and_add(x, axis):
+    parts = lax.all_gather(x, axis, axis=0, tiled=False)
+    result = parts.sum(axis=0)
+    return result
 
 
 def extended_2(value, sides, width):
@@ -83,7 +89,7 @@
     short_range = grouped(repulsion_kernel, targets, (gather_local(extended, neighbors),)).reshape(
         3, atom_dev
     )
-    centroid = lax.psum(coords, "bead") / beads
+    centroid = gather_and_add(coords, "bead") / beads
     with_charge = jnp.concatenate([centroid, charges[None]], axis=0)
     cent_ext = extended_2(with_charge, (("space", 1),), rim_width)
     cent_tiles = centroid.reshape(3, tiles_domain, TILE)

time: 1030 us -> 976 us (0.948)
  waiting for transfers between devices: 156 us -> 103 us
    psum x1 -> x0, waiting for transfers between devices: 145 us -> none  [per_device(): centroid = lax.psum(coords, 'bead') / beads]
    all_gather x0 -> x1, waiting for transfers between devices: none -> 95.8 us  [gather_and_add(): parts = lax.all_gather(x, axis, axis=0, tiled=False)]
  transfers between devices with their start and end apart: 15 -> 15, of which waited for: 5 -> 5; matrix products, arithmetic and copies ran while one was open for 55% -> 58% of each run, Pallas kernels for 0% -> 0%
where the time goes in v1:
time: 976 us; the launch traced here: 964 us
  other arithmetic  591 us (61%)
  local copies, waits for them, and re-layouts  228 us (23%)
  waiting for transfers between devices  103 us (11%)
  starting transfers between devices  18 us (2%)
  between operations  14.6 us (1%)
    reduce_sum x128, other arithmetic, dipole_kernel(): jnp.sum(weight[None] * (0.25 * displace * projected[None] - 0.5 * spread_...  199 us
    reduce_sum x128, other arithmetic, dipole_kernel(): weight = jnp.exp(-0.25 * jnp.sum(displace * displace, axis=0))  135 us
    exp x128, other arithmetic, dipole_kernel(): weight = jnp.exp(-0.25 * jnp.sum(displace * displace, axis=0))  119 us
    sub x256, local copies, waits for them, and re-layouts, dipole_kernel(): displace = targets[:, :, :, None] - sources[:, :, None, :]  105 us
    all_gather x1, waiting for transfers between devices, gather_and_add(): parts = lax.all_gather(x, axis, axis=0, tiled=False)  95.8 us
    sub x64, local copies, waits for them, and re-layouts, repulsion_kernel(): displace = targets[:, :, :, None] - sources[:, :, None, :]  48 us
    gather x8, local copies, waits for them, and re-layouts, gather_local(): picked = jnp.take(tiles, tile_rows, axis=1)  29.6 us
    reduce_sum x32, other arithmetic, charge_kernel(): return jnp.sum(weight[None] * displace, axis=3)  27.5 us
  transfers between devices with their start and end apart: 15, of which 5 were waited for; matrix products, arithmetic and copies ran while one was open for 58% of the time, Pallas kernels for 0%

profile of v1, /device:TPU:7, one launch (start us, length us, event | category | flops | bytes accessed | tf_op | source)
XLA Modules:
  0.0 963.9 jit_solution(5654028894666897079)
XLA Ops:
  9.7 2.5 collective-permute-start
  14.9 95.8 %all-gather.2.cloned.1.call-done = f32[32,3,16384]{2,1,0:T(4,128)} async-done(((f32[1,3,16384]{2,1,0:T(4,128)}), f32[32,3,16384]{2,1,0:T(4,128)}) %all-gather.2.cloned.1.call-update) | async-done | bytes 6291472 | tf_op jit(solution)/shard_map/all_gather | solution.py:15
  110.6 4.8 reduce_sum.153
  117.1 3.6 gather_fusion.1
  121.6 2.8 gather_fusion
  125.4 8.0 gather_fusion.2
  133.4 3.6 fusion.29
  140.4 87.0 %while.61 = (s32[]{:T(128)}, f32[32,3,4,128]{3,2,1,0:T(4,128)S(1)}, f32[32,3,4,128]{3,2,1,0:T(4,128)S(1)}, f32[32,3,4,1024]{3,2,1,0:T(4,128)}, f32[32,1,4,1024]{3,2,1,0:T(4,128)S(1)}, /*index=5*/s32[]{:T(128)}) while((s32[]{:T(128)}, f32[32,3,4,128]{3,2,1,0:T(4,128)S(1)}, f32[32,3,4,128]{3,2,1,0:T(4,128)S(1)}, f32[32,3,4,1024]{3,2,1,0:T(4,128)}, ...), condition=%wide.region_8.10_spmd, body=%wide.region_5.9_spmd.sunk | while | flops 9959938 | bytes 8677469 | solution.py:65
  227.7 2.6 collective-permute-start.6
  231.1 3.5 collective-permute-done.7
  234.6 3.6 gather_fusion.3
  241.4 141.8 %while.62 = (s32[]{:T(128)}, f32[32,3,4,128]{3,2,1,0:T(4,128)S(1)}, f32[32,3,4,128]{3,2,1,0:T(4,128)S(1)}, f32[32,3,4,1024]{3,2,1,0:T(4,128)}, f32[32,3,4,1024]{3,2,0,1:T(4,128)S(1)}, /*index=5*/s32[]{:T(128)}) while((s32[]{:T(128)}, f32[32,3,4,128]{3,2,1,0:T(4,128)S(1)}, f32[32,3,4,128]{3,2,1,0:T(4,128)S(1)}, ...), condition=%wide.region_13.15_spmd, body=%wide.region_9.14_spmd.sunk | while | flops 15739394 | bytes 17262684 | solution.py:65
  384.1 4.8 collective-permute-start.3
  389.0 3.6 gather_fusion.4
  395.8 141.8 %while.63 = (s32[]{:T(128)}, f32[32,3,4,128]{3,2,1,0:T(4,128)S(1)}, f32[32,3,4,128]{3,2,1,0:T(4,128)S(1)}, f32[32,3,4,1024]{3,2,1,0:T(4,128)}, f32[32,3,4,1024]{3,2,0,1:T(4,128)S(1)}, /*index=5*/s32[]{:T(128)}) while((s32[]{:T(128)}, f32[32,3,4,128]{3,2,1,0:T(4,128)S(1)}, f32[32,3,4,128]{3,2,1,0:T(4,128)S(1)}, ...), condition=%wide.region_18.20_spmd, body=%wide.region_14.19_spmd.sunk | while | flops 15739394 | bytes 17262684 | solution.py:65
  537.9 3.1 collective-permute-start.10
  542.7 2.6 collective-permute-done.11
  545.3 3.6 gather_fusion.5
  552.1 141.8 %while.64 = (s32[]{:T(128)}, f32[32,3,4,128]{3,2,1,0:T(4,128)S(1)}, f32[32,3,4,128]{3,2,1,0:T(4,128)S(1)}, f32[32,3,4,1024]{3,2,1,0:T(4,128)}, f32[32,3,4,1024]{3,2,0,1:T(4,128)S(1)}, /*index=5*/s32[]{:T(128)}) while((s32[]{:T(128)}, f32[32,3,4,128]{3,2,1,0:T(4,128)S(1)}, f32[32,3,4,128]{3,2,1,0:T(4,128)S(1)}, ...), condition=%wide.region_23.25_spmd, body=%wide.region_19.24_spmd.sunk | while | flops 15739394 | bytes 17262684 | solution.py:65
  694.8 3.0 collective-permute-start.12
  697.8 107.9 %while.60 = (s32[]{:T(128)}, f32[32,3,4,128]{3,2,1,0:T(4,128)S(1)}, f32[32,3,4,128]{3,2,0,1:T(4,128)}, f32[32,3,4,1024]{3,2,0,1:T(4,128)}, s32[]{:T(128)}) while((s32[]{:T(128)}, f32[32,3,4,128]{3,2,1,0:T(4,128)S(1)}, f32[32,3,4,128]{3,2,0,1:T(4,128)}, f32[32,3,4,1024]{3,2,0,1:T(4,128)}, s32[]{:T(128)}) %tuple.172), condition=%wide.region_3.5_spmd, body=%wide.region_0.4_spmd.sunk | while | flops 9437186 | bytes 8628305 | solution.py:65
  805.9 3.6 gather_fusion.6
  812.7 142.0 %while.65 = (s32[]{:T(128)}, f32[32,3,4,128]{3,2,1,0:T(4,128)S(1)}, f32[32,3,4,128]{3,2,1,0:T(4,128)S(1)}, f32[32,3,4,1024]{3,2,1,0:T(4,128)}, f32[32,3,4,1024]{3,2,0,1:T(4,128)S(1)}, /*index=5*/s32[]{:T(128)}) while((s32[]{:T(128)}, f32[32,3,4,128]{3,2,1,0:T(4,128)S(1)}, f32[32,3,4,128]{3,2,1,0:T(4,128)S(1)}, ...), condition=%wide.region_28.30_spmd, body=%wide.region_24.29_spmd.sunk | while | flops 15739394 | bytes 17262684 | solution.py:65
  954.8 2.2 multiply_add_fusion
  (1409 shorter events, 783.1 us)
Async XLA Ops:
  7.2 103.5 %all-gather.2.cloned.1.call-start = ((), (), s32[]{:S(2)}) async-start(), calls=%async_computation | async-start | bytes 8650752 | tf_op jit(solution)/shard_map/all_gather | solution.py:15
  9.7 107.3 %collective-permute-start = (f32[3,512]{1,0:T(4,128)S(1)}, f32[3,512]{1,0:T(4,128)S(1)}, u32[]{:S(2)}, u32[]{:S(2)}) collective-permute-start(f32[3,512]{1,0:T(4,128)S(1)} %get-tuple-element.340), channel_id=1, source_target_pairs={{0,1},{1,2},{2,3},{3,4},{4,5},{5,6},{6,7},{7,0},{8,9},{9,10},{10,1... | collective-permute-start | bytes 18440 | tf_op jit(solution)/shard_map/ppermute | solution.py:27
  12.2 104.9 %collective-permute-start.1 = (f32[3,512]{1,0:T(4,128)S(1)}, f32[3,512]{1,0:T(4,128)S(1)}, u32[]{:S(2)}, u32[]{:S(2)}) collective-permute-start(f32[3,512]{1,0:T(4,128)S(1)} %get-tuple-element.341), channel_id=1, source_target_pairs={{1,0},{2,1},{3,2},{4,3},{5,4},{6,5},{7,6},{0,7},{9,8},{10,9},{11,1... | collective-permute-start | bytes 18440 | tf_op jit(solution)/shard_map/ppermute | solution.py:28
  14.9 100.6 %copy-start.3 = (f32[16384]{0:T(1024)S(1)}, f32[16384]{0:T(1024)}, u32[]{:S(2)}) copy-start(f32[16384]{0:T(1024)} %param.20) | copy-start | bytes 196612
  14.9 102.2 %copy-start.1 = (f32[1,3,16384]{2,1,0:T(4,128)S(1)}, f32[1,3,16384]{2,1,0:T(4,128)}, u32[]{:S(2)}) copy-start(f32[1,3,16384]{2,1,0:T(4,128)} %copy.179) | copy-start | bytes 589828
  115.5 5.5 collective-permute-start.4
  117.1 4.3 collective-permute-start.5
  138.8 1.3 copy-start.2
  138.8 1.3 copy-start.5
  140.4 87.2 %copy-start.4 = (f32[16384]{0:T(1024)S(1)}, f32[16384]{0:T(1024)}, u32[]{:S(2)}) copy-start(f32[16384]{0:T(1024)} %param.21) | copy-start | bytes 196612
  227.7 3.4 collective-permute-start.6
  230.3 4.3 collective-permute-start.7
  383.6 5.3 collective-permute-start.8
  383.6 5.3 collective-permute-start.9
  384.1 570.7 %collective-permute-start.2 = (f32[1,3,16384]{2,0,1:T(1,128)}, f32[1,3,16384]{2,0,1:T(1,128)S(1)}, u32[]{:S(2)}, u32[]{:S(2)}) collective-permute-start(f32[1,3,16384]{2,0,1:T(1,128)} %param.19), channel_id=1, source_target_pairs={{0,8},{8,16},{16,24},{24,32},{32,40},{40,48},{48,56},{56,64},{64,7... | collective-permute-start | bytes 589832 | tf_op jit(solution)/shard_map/ppermute | solution.py:27
  384.1 570.7 %collective-permute-start.3 = (f32[1,3,16384]{2,0,1:T(1,128)}, f32[1,3,16384]{2,0,1:T(1,128)}, u32[]{:S(2)}, u32[]{:S(2)}) collective-permute-start(f32[1,3,16384]{2,0,1:T(1,128)} %param.19), channel_id=1, source_target_pairs={{8,0},{16,8},{24,16},{32,24},{40,32},{48,40},{56,48},{64,56},{72,6... | collective-permute-start | bytes 589832 | tf_op jit(solution)/shard_map/ppermute | solution.py:28
  395.8 145.2 %copy-start.6 = (f32[16384]{0:T(1024)S(1)}, f32[16384]{0:T(1024)}, u32[]{:S(2)}) copy-start(f32[16384]{0:T(1024)} %param.22) | copy-start | bytes 196612
  537.6 3.4 copy-start
  537.9 4.7 collective-permute-start.10
  541.0 4.3 collective-permute-start.11
  694.8 111.0 %collective-permute-start.13 = (f32[3,512]{1,0:T(4,128)S(1)}, f32[3,512]{1,0:T(4,128)S(1)}, u32[]{:S(2)}, u32[]{:S(2)}) collective-permute-start(f32[3,512]{1,0:T(4,128)S(1)} %get-tuple-element.338), channel_id=1, source_target_pairs={{1,0},{2,1},{3,2},{4,3},{5,4},{6,5},{7,6},{0,7},{9,8},{10,9},{11,1... | collective-permute-start | bytes 18440 | tf_op jit(solution)/shard_map/ppermute | solution.py:28
  694.8 111.0 %collective-permute-start.12 = (f32[3,512]{1,0:T(4,128)S(1)}, f32[3,512]{1,0:T(4,128)S(1)}, u32[]{:S(2)}, u32[]{:S(2)}) collective-permute-start(f32[3,512]{1,0:T(4,128)S(1)} %get-tuple-element.339), channel_id=1, source_target_pairs={{0,1},{1,2},{2,3},{3,4},{4,5},{5,6},{6,7},{7,0},{8,9},{9,10},{10,1... | collective-permute-start | bytes 18440 | tf_op jit(solution)/shard_map/ppermute | solution.py:27
Sparse Core Ops, SparseCore 0:
  10.6 100.0 all-gather.1
